TPU v7x, 256 devices: a whole 4x4x8 slice. The times are simulated.
256 devices in a mesh: dp: 16 (over z_hi, x), rows: 16 (over y, z_lo, core).
Axes of the slice: x: 4, y: 4, z: 8 (z_hi: 4, z_lo: 2; z = z_hi * 2 + z_lo), core: 2. Of those that a mesh axis runs over, the one named last changes fastest.
Arguments:
- features: bfloat16 [16, 128, 32, 1536], P('dp', 'rows'), may hold values from -6 to 6
- kernel: bfloat16 [7, 7, 1536], replicated, may hold values from -0.875 to 0.875
- ln_gain: float32 [1536], replicated, may hold values from 0.1 to 1.9
- layer_scale: float32 [1536], replicated, may hold values from 0.2 to 1
- w_in: bfloat16 [1536, 3072], P(('dp', 'rows')), may hold values from -0.15625 to 0.15625
- w_out: bfloat16 [3072, 1536], P(('dp', 'rows')), may hold values from -0.109375 to 0.109375
- pairs: int32 [16], replicated, may hold values from 0 to 15, as said below
- negatives: int32 [16, 32, 8, 8], P('dp', 'rows'), may hold values from 0 to 127
Outputs:
- grad_features: bfloat16 [16, 128, 32, 1536], P('dp', 'rows')
- grad_kernel: float32 [7, 7, 1536], replicated
- loss: float32 [], replicated
Inputs may be any that keep to these rules, and one draw needn't show every extreme that they name: pairs[pairs[i]] == i and pairs[i] != i: the images form 16 / 2 preference pairs.
All inputs are finite; a program needn't handle non-finite values.
Results may differ from a plain program's by a relative error of at most 0.014.
Values may be sent and summed in bfloat16 or wider, within the bound.
No kernel may reach another device: no remote copies, remote signals or barrier semaphores. Data moves between devices by JAX's collectives and lax.ppermute only.
A program may use at most 128 MiB of HBM per device.

v0:
```python
import jax
import jax.numpy as jnp
from jax import lax
from jax.sharding import PartitionSpec as P

REGION = 4
NEG = 8
loss_scale = 1024.0
inv_temp = 16.0
eps_layer = 1e-06
eps_norm = 1e-06


def padded_2(cells, sides, width):
    for axis, dim in sides:
        count = lax.axis_size(axis)
        ends = count - 1
        head = lax.slice_in_dim(cells, 0, width, axis=dim)
        tail = lax.slice_in_dim(cells, cells.shape[dim] - width, cells.shape[dim], axis=dim)
        cells = jnp.concatenate(
            [
                lax.ppermute(tail, axis, [(i, (i + 1) % count) for i in range(ends)]),
                cells,
                lax.ppermute(head, axis, [((i + 1) % count, i) for i in range(ends)]),
            ],
            axis=dim,
        )
    return cells


def depthwise(padded, kernel, height, breadth):
    summed = jnp.zeros((padded.shape[0], height, breadth, padded.shape[3]), jnp.float32)
    for offset_row in range(7):
        for offset_col in range(7):
            window = padded[
                :, offset_row : offset_row + height, offset_col : offset_col + breadth, :
            ]
            summed = summed + window.astype(jnp.float32) * kernel[offset_row, offset_col].astype(
                jnp.float32
            )
    return summed


def kernel_terms(padded, grad_conv, height, breadth):
    grad_float = grad_conv.astype(jnp.float32)
    stacked = []
    for offset_row in range(7):
        row_terms = []
        for offset_col in range(7):
            window = padded[
                :, offset_row : offset_row + height, offset_col : offset_col + breadth, :
            ]
            row_terms.append(jnp.sum(window.astype(jnp.float32) * grad_float, axis=(0, 1, 2)))
        stacked.append(jnp.stack(row_terms))
    return jnp.stack(stacked)


def gelu_parts(pre_act):
    normal_cdf = 0.5 * (1.0 + jax.scipy.special.erf(pre_act * 0.7071067811865476))
    density = jnp.exp(-0.5 * pre_act * pre_act) * 0.3989422804014327
    return (pre_act * normal_cdf, normal_cdf + pre_act * density)


def norm_rows(conv_rows):
    centred = conv_rows - jnp.mean(conv_rows, axis=-1, keepdims=True)
    spread = jnp.sqrt(jnp.mean(centred * centred, axis=-1, keepdims=True) + eps_layer)
    return (centred / spread, spread)


def body(features, kernel, ln_gain, layer_scale, w_in, w_out, pairs, negatives):
    height, breadth, channels = (features.shape[1], features.shape[2], features.shape[3])
    w_in_all, w_out_all = (
        lax.all_gather(w_in, ("dp", "rows"), axis=0, tiled=True),
        lax.all_gather(w_out, ("dp", "rows"), axis=0, tiled=True),
    )
    rimmed = padded_2(features, (("rows", 1),), 3)
    padded = jnp.pad(rimmed, ((0, 0), (0, 0), (3, 3), (0, 0)))
    conv_rows = depthwise(padded, kernel, height, breadth).reshape(-1, channels)
    unit_rows, spread = norm_rows(conv_rows)
    normed = (unit_rows * ln_gain).astype(jnp.bfloat16)
    pre_act = jnp.dot(normed, w_in_all, preferred_element_type=jnp.float32)
    activated, gelu_slope = gelu_parts(pre_act)
    hidden = activated.astype(jnp.bfloat16)
    mixed_rows = jnp.dot(hidden, w_out_all, preferred_element_type=jnp.float32)
    block_out = features.reshape(-1, channels).astype(jnp.float32) + layer_scale * mixed_rows
    reg_rows, reg_cols = (height // REGION, breadth // REGION)
    pooled = jnp.mean(block_out.reshape(reg_rows, REGION, reg_cols, REGION, channels), axis=(1, 3))
    inv_norm = lax.rsqrt(jnp.sum(pooled * pooled, axis=-1, keepdims=True) + eps_norm)
    unit_tok = pooled * inv_norm
    tokens_b = unit_tok.astype(jnp.bfloat16)
    gathered = lax.all_gather(tokens_b[None], "dp", axis=0, tiled=True)
    images = gathered.shape[0]
    keys_flat = gathered.transpose(1, 0, 2, 3).reshape(reg_rows, images * reg_cols, channels)
    my_image = lax.axis_index("dp")
    partner = lax.dynamic_index_in_dim(pairs, my_image, keepdims=False)
    columns = jnp.arange(reg_cols, dtype=jnp.int32)
    positive = jnp.broadcast_to(
        (partner * reg_cols + columns)[None, :, None], (reg_rows, reg_cols, 1)
    )
    chosen = jnp.concatenate([positive, negatives[0]], axis=2)
    one_hot = (chosen[..., None] == jnp.arange(images * reg_cols, dtype=jnp.int32)).astype(
        jnp.float32
    )
    similar = jnp.einsum("rtc,rjc->rtj", tokens_b, keys_flat, preferred_element_type=jnp.float32)
    logits = inv_temp * jnp.sum(one_hot * similar[:, :, None, :], axis=-1)
    exp_logits = jnp.exp(logits)
    denominator = jnp.sum(exp_logits, axis=-1, keepdims=True)
    loss_tok = jnp.log(denominator[..., 0]) - logits[..., 0]
    first_slot = (jnp.arange(NEG + 1) == 0).astype(jnp.float32)
    slot_coef = loss_scale * inv_temp * (exp_logits / denominator - first_slot)
    weight_map = jnp.sum(slot_coef[..., None] * one_hot, axis=2)
    anchor = jnp.einsum(
        "rtj,rjc->rtc", weight_map, keys_flat.astype(jnp.float32), precision=lax.Precision.HIGHEST
    )
    weight_four = weight_map.reshape(reg_rows, reg_cols, images, reg_cols)
    key_table = jnp.einsum(
        "rtiu,rtc->iruc", weight_four, tokens_b.astype(jnp.float32), precision=lax.Precision.HIGHEST
    )
    own_grads = lax.psum_scatter(
        key_table.astype(jnp.bfloat16), "dp", scatter_dimension=0, tiled=True
    ).astype(jnp.float32)[0]
    grad_tok = anchor + own_grads
    grad_pool = (
        grad_tok - unit_tok * jnp.sum(unit_tok * grad_tok, axis=-1, keepdims=True)
    ) * inv_norm
    scaled = grad_pool / float(REGION * REGION)
    grad_out = jnp.broadcast_to(
        scaled[:, None, :, None, :], (reg_rows, REGION, reg_cols, REGION, channels)
    ).reshape(height * breadth, channels)
    grad_mix = (layer_scale * grad_out).astype(jnp.bfloat16)
    grad_hid = lax.dot_general(
        grad_mix, w_out_all, (((1,), (1,)), ((), ())), preferred_element_type=jnp.float32
    )
    grad_pre = (grad_hid * gelu_slope).astype(jnp.bfloat16)
    grad_norm = lax.dot_general(
        grad_pre, w_in_all, (((1,), (1,)), ((), ())), preferred_element_type=jnp.float32
    )
    grad_unit = grad_norm * ln_gain
    mean_one = jnp.mean(grad_unit, axis=-1, keepdims=True)
    mean_two = jnp.mean(grad_unit * unit_rows, axis=-1, keepdims=True)
    grad_conv = (
        ((grad_unit - mean_one - unit_rows * mean_two) / spread)
        .astype(jnp.bfloat16)
        .reshape(1, height, breadth, channels)
    )
    flipped = kernel[::-1, ::-1]
    grad_rim = padded_2(grad_conv, (("rows", 1),), 3)
    grad_pad = jnp.pad(grad_rim, ((0, 0), (0, 0), (3, 3), (0, 0)))
    conv_back = depthwise(grad_pad, flipped, height, breadth)
    grad_features = (grad_out.reshape(1, height, breadth, channels) + conv_back).astype(
        jnp.bfloat16
    )
    kernel_local = kernel_terms(padded, grad_conv, height, breadth)
    grad_kernel, loss_sum = lax.psum((kernel_local, jnp.sum(loss_tok)), ("dp", "rows"))
    token_count = lax.axis_size("dp") * lax.axis_size("rows") * reg_rows * reg_cols
    loss = loss_sum / float(token_count)
    return (grad_features, grad_kernel, loss)


def solution(mesh):
    return jax.shard_map(
        body,
        mesh=mesh,
        in_specs=(
            P("dp", "rows", None, None),
            P(),
            P(),
            P(),
            P(("dp", "rows"), None),
            P(("dp", "rows"), None),
            P(),
            P("dp", "rows", None, None),
        ),
        out_specs=(P("dp", "rows", None, None), P(), P()),
        check_vma=False,
    )
```

profile of v0, /device:TPU:1, one launch (start us, length us, event | category | flops | bytes accessed | tf_op | source)
XLA Modules:
  0.0 1320.9 jit_solution(3228387225316494650)
XLA Ops:
  7.2 0.7 all-gather.5.cloned.1.call-update
  8.0 0.7 all-gather.7.cloned.1.call-update
  8.7 1.1 fusion.161
  9.8 4.9 collective-permute-start
  14.7 1.9 collective-permute-start.1
  16.7 1.2 dynamic_slice.4
  18.7 0.8 pad_add_fusion
  19.4 1.2 convert_reduce_fusion.46
  20.6 0.5 compare_convert_fusion
  21.1 0.1 copy.22
  21.2 0.3 convert_reduce_fusion.48
  21.7 0.3 convert_reduce_fusion.47
  22.2 0.1 constant_dynamic-update-slice_fusion
  22.4 0.5 collective-permute-done.1
  22.9 0.7 copy-done.5
  23.6 0.5 select_maximum_fusion.2
  24.4 13.8 %fusion.158 = (f32[8,32]{1,0:T(8,128)S(1)}, f32[1,8,32,1536]{3,2,1,0:T(8,128)}) fusion(f32[1536]{0:T(1024)S(1)} %get-tuple-element.110, bf16[1,14,38,1536]{3,2,1,0:T(8,128)(2,1)S(1)} %select_maximum_fusion.2, f32[1536]{0:T(1024)S(1)} %get-tuple-element.111, f32[1536]{0:T(1024)S(1)} %get-tuple-element.64, f32[1536]{0:T(1024)S(1)} %get-tuple-element.65, ...), kind=kLoop, calls=%fused_computation.367 | loop fusion | flops 57802496 | bytes 40410112 | tf_op jit(solution)/shard_map/reduce_sum | solution.py:65
  38.2 0.1 div.50
  38.3 1.7 multiply_reduce_fusion.1
  40.0 0.1 sqrt.12
  40.1 2.8 fusion.136
  42.9 392.4 %all-gather.5.cloned.1.call-done = bf16[256,6,3072]{2,1,0:T(8,128)(2,1)} async-done(((bf16[1,6,3072]{2,1,0:T(8,128)(2,1)}), bf16[256,6,3072]{2,1,0:T(8,128)(2,1)}) %all-gather.5.cloned.1.call-update) | async-done | bytes 9437200 | tf_op jit(solution)/shard_map/all_gather | solution.py:73
  435.3 14.2 %reshape.776 = bf16[1536,3072]{1,0:T(8,128)(2,1)} reshape(bf16[256,6,3072]{2,1,0:T(8,128)(2,1)} %all-gather.5.cloned.1.call-done) | data formatting | bytes 18874368
  449.5 8.5 fusion.141
  458.0 399.4 %all-gather.7.cloned.1.call-done = bf16[256,12,1536]{2,1,0:T(8,128)(2,1)} async-done(((bf16[1,12,1536]{2,1,0:T(8,128)(2,1)}), bf16[256,12,1536]{2,1,0:T(8,128)(2,1)}) %all-gather.7.cloned.1.call-update) | async-done | bytes 9437200 | tf_op jit(solution)/shard_map/all_gather | solution.py:74
  857.4 15.0 %reshape.778 = bf16[3072,1536]{1,0:T(8,128)(2,1)} reshape(bf16[256,12,1536]{2,1,0:T(8,128)(2,1)} %all-gather.7.cloned.1.call-done) | data formatting | bytes 18874368
  872.4 8.5 fusion.7
  880.9 2.7 reshape.719
  883.6 1.8 reduce_sum.544
  885.4 0.1 multiply_reduce_fusion.2
  885.5 0.1 fusion.150
  885.6 36.9 %all_gather.11 = bf16[16,2,8,1536]{3,2,1,0:T(8,128)(2,1)S(1)} all-gather(bf16[1,2,8,1536]{3,2,1,0:T(8,128)(2,1)S(1)} %fusion.150), channel_id=1, replica_groups=mesh['dp'=16,'rows'=16] {'dp'}, dimensions={0}, use_global_device_ids=true | all-gather | bytes 835584 | tf_op jit(solution)/shard_map/all_gather | solution.py:91
  922.5 0.9 copy-done.7
  923.4 0.3 fusion.143
  923.7 0.2 select_reduce_fusion.1
  924.0 0.1 select_reduce_fusion
  924.1 0.1 reshape.721
  924.3 1.7 fusion.8
  926.0 0.2 all-reduce.4.cloned.1.call-start
  926.2 0.6 subtract_reduce_fusion
  926.8 84.5 %psum.15 = f32[]{:T(128)} all-reduce(f32[]{:T(128)} %subtract_reduce_fusion), channel_id=1, replica_groups=mesh['dp'=16,'rows'=16] {'dp','rows'}, use_global_device_ids=true, to_apply=%region_62.63 | all-reduce | flops 1 | bytes 8 | tf_op jit(solution)/shard_map/psum | solution.py:154
  1012.0 6.6 reduce-scatter.2.cloned.1.call-done
  1018.6 1.6 convolution_add_fusion
  1020.2 0.3 fusion.12
  1020.5 1.4 broadcast_in_dim.5
  1021.9 2.8 reshape.722
  1024.7 2.8 reshape_reshape.3
  1027.4 12.4 fusion.157
  1039.9 6.2 fusion.135
  1046.1 2.5 fusion.132
  1048.6 4.0 fusion.114
  1053.3 0.1 stack.199
  1053.4 1.1 fusion.160
  1054.5 4.8 collective-permute-start.2
  1059.4 2.1 collective-permute-start.3
  1061.5 0.1 stack.208
  1061.7 0.1 stack.226
  1061.8 0.1 stack.235
  1062.1 0.7 copy-done.10
  1063.1 5.5 collective-permute-done.3
  1068.6 0.5 select_maximum_fusion
  1069.5 12.2 add_convert_fusion
  1081.6 229.9 %all-reduce.4.cloned.1.call-done = f32[7,7,1536]{2,1,0:T(8,128)} async-done(((f32[7,7,1536]{2,1,0:T(8,128)}), f32[7,7,1536]{2,1,0:T(8,128)}) %all-reduce.4.cloned.1.call-update) | async-done | bytes 301072 | tf_op jit(solution)/shard_map/psum | solution.py:154
  1311.5 1.7 copy.48
  (226 shorter events, 1.3 us)
Async XLA Ops:
  7.2 15.0 %copy-start.4 = (bf16[1,8,32,1536]{3,2,1,0:T(8,128)(2,1)S(1)}, bf16[1,8,32,1536]{3,2,1,0:T(8,128)(2,1)}, u32[]{:S(2)}) copy-start(bf16[1,8,32,1536]{3,2,1,0:T(8,128)(2,1)} %param.8) | copy-start | bytes 2359300
  7.2 14.0 %copy-start.9 = (bf16[7,7,1536]{2,1,0:T(8,128)(2,1)S(1)}, bf16[7,7,1536]{2,1,0:T(8,128)(2,1)}, u32[]{:S(2)}) copy-start(bf16[7,7,1536]{2,1,0:T(8,128)(2,1)} %param.9) | copy-start | bytes 451588
  7.2 428.1 %all-gather.5.cloned.1.call-start = ((), (), s32[]{:S(2)}) async-start(), calls=%async_computation.3 | async-start | bytes 12632064 | tf_op jit(solution)/shard_map/all_gather | solution.py:73
  7.9 849.5 %all-gather.7.cloned.1.call-start = ((), (), s32[]{:S(2)}) async-start(), calls=%async_computation.4 | async-start | bytes 12632064 | tf_op jit(solution)/shard_map/all_gather | solution.py:74
  8.7 1009.9 %reduce-scatter.2.cloned.1.call-start = ((), (), s32[]{:S(2)}) async-start(), calls=%async_computation.1 | async-start | bytes 835584 | tf_op jit(solution)/shard_map/reduce_scatter | solution.py:119
  9.8 12.4 collective-permute-start
  14.7 8.1 collective-permute-start.1
  21.5 2.6 copy-start.11
  21.5 2.6 copy-start.13
  21.6 2.6 copy-start.15
  21.6 2.6 copy-start.17
  21.6 2.6 copy-start.19
  21.6 2.6 copy-start.21
  21.6 2.6 copy-start.23
  21.6 2.6 copy-start.25
  21.6 2.6 copy-start.27
  21.6 2.6 copy-start.29
  21.6 2.6 copy-start.31
  21.6 2.6 copy-start.33
  22.0 2.3 copy-start.35
  22.0 2.3 copy-start.37
  22.0 2.3 copy-start.39
  42.9 406.6 %copy-start.74 = (f32[1536]{0:T(1024)S(1)}, f32[1536]{0:T(1024)}, u32[]{:S(2)}) copy-start(f32[1536]{0:T(1024)} %param.10) | copy-start | bytes 18436
  458.0 414.4 %copy-start.75 = (f32[1536]{0:T(1024)S(1)}, f32[1536]{0:T(1024)}, u32[]{:S(2)}) copy-start(f32[1536]{0:T(1024)} %param.11) | copy-start | bytes 18436
  883.6 40.3 %copy-start.73 = (f32[9]{0:T(128)S(1)}, f32[9]{0:T(128)}, u32[]{:S(2)}) copy-start(f32[9]{0:T(128)} %compare_convert_fusion) | copy-start | bytes 112
  926.0 385.5 %all-reduce.4.cloned.1.call-start = ((), (), s32[]{:S(2)}) async-start(), calls=%async_computation.2 | async-start | bytes 688128 | tf_op jit(solution)/shard_map/psum | solution.py:154
  1039.9 6.2 copy-start.3
  1039.9 6.2 copy-start.6
  1046.1 2.6 copy-start
  1053.1 15.6 %copy-start.1 = (bf16[256,1536]{1,0:T(8,128)(2,1)S(1)}, bf16[256,1536]{1,0:T(8,128)(2,1)}, u32[]{:S(2)}) copy-start(bf16[256,1536]{1,0:T(8,128)(2,1)} %copy-done) | copy-start | bytes 2359300
  1054.5 8.6 collective-permute-start.2
  1059.4 9.3 collective-permute-start.3
  1062.8 6.3 copy-start.8
  1062.8 6.3 copy-start.12
  1062.8 6.3 copy-start.14
  1062.8 6.3 copy-start.16
  1062.9 6.3 copy-start.18
  1062.9 6.3 copy-start.20
  1062.9 6.3 copy-start.22
  1062.9 6.3 copy-start.24
  1062.9 6.3 copy-start.26
  1062.9 6.3 copy-start.28
  1062.9 6.3 copy-start.30
  1062.9 6.3 copy-start.32
  1062.9 6.3 copy-start.34
  1062.9 6.3 copy-start.36
  1063.0 6.3 copy-start.38
  1063.0 6.3 copy-start.40
  1063.0 6.3 copy-start.42
  1063.0 6.3 copy-start.44
  1063.0 6.3 copy-start.46
  1063.0 6.3 copy-start.48
  1063.0 6.3 copy-start.50
  1063.0 6.3 copy-start.52
  1063.0 6.3 copy-start.54
  1063.0 6.3 copy-start.56
  1063.1 6.3 copy-start.58
  1063.1 6.3 copy-start.60
  1063.1 6.3 copy-start.62
  1063.1 6.3 copy-start.64
  1063.1 6.3 copy-start.66
  1063.1 6.3 copy-start.68
  1063.1 6.3 copy-start.70
  1063.1 6.3 copy-start.72
  (20 other events, 41.3 us)
Sparse Core Ops, SparseCore 0:
  9.9 425.3 all-gather.4
  437.2 420.2 all-gather.6
  926.1 92.4 reduce-scatter.1
  1062.9 248.5 all-reduce.3
where the time goes:
time: 1320 us
  waiting for transfers between devices  1040 us (79%)
  blocking collectives  121 us (9%)
  other arithmetic  50.6 us (4%)
  local copies, waits for them, and re-layouts  48.1 us (4%)
  matrix products  33 us (2%)
  between operations  17.9 us (1%)
  starting transfers between devices  14.2 us (1%)
    all_gather x1, waiting for transfers between devices, body(): lax.all_gather(w_out, ('dp', 'rows'), axis=0, tiled=True)  399 us
    all_gather x1, waiting for transfers between devices, body(): lax.all_gather(w_in, ('dp', 'rows'), axis=0, tiled=True)  392 us
    psum x1, waiting for transfers between devices, body(): lax.psum((kernel_local, jnp.sum(loss_tok)), ('dp', 'rows'))  230 us
    psum x1, blocking collectives, body(): lax.psum((kernel_local, jnp.sum(loss_tok)), ('dp', 'rows'))  84.5 us
    all_gather x1, blocking collectives, body(): gathered = lax.all_gather(tokens_b[None], 'dp', axis=0, tiled=True)  36.9 us
    unnamed x162, local copies, waits for them, and re-layouts  33.6 us
  transfers between devices with their start and end apart: 8, of which 6 were waited for; matrix products, arithmetic and copies ran while one was open for 5% of the time, Pallas kernels for 0%

commit v1 on v0

--- a/solution.py
+++ b/solution.py
@@ -9,6 +9,13 @@
 inv_temp = 16.0
 eps_layer = 1e-06
 eps_norm = 1e-06
+
+
+def exchange_gather(x, mesh_axis, d):
+    peers = lax.axis_size(mesh_axis)
+    blocks = jnp.stack([x for _ in range(peers)])
+    blocks = lax.all_to_all(blocks, mesh_axis, split_axis=0, concat_axis=0)
+    return jnp.concatenate(blocks, axis=d)
 
 
 def padded_2(cells, sides, width):
@@ -71,7 +78,7 @@
     height, breadth, channels = (features.shape[1], features.shape[2], features.shape[3])
     w_in_all, w_out_all = (
         lax.all_gather(w_in, ("dp", "rows"), axis=0, tiled=True),
-        lax.all_gather(w_out, ("dp", "rows"), axis=0, tiled=True),
+        exchange_gather(w_out, ("dp", "rows"), 0),
     )
     rimmed = padded_2(features, (("rows", 1),), 3)
     padded = jnp.pad(rimmed, ((0, 0), (0, 0), (3, 3), (0, 0)))

time: 1320 us -> 1070 us (0.81)
  waiting for transfers between devices: 1040 us -> 695 us
  local copies, waits for them, and re-layouts: 48.1 us -> 99.9 us
  starting transfers between devices: 14.2 us -> 29.9 us
  blocking collectives: 121 us -> 135 us
    all_gather x1 -> x0, waiting for transfers between devices: 399 us -> none  [body(): lax.all_gather(w_out, ('dp', 'rows'), axis=0, tiled=True)]
    ppermute x2, waiting for transfers between devices: 0.01 us -> 303 us  [padded_2(): lax.ppermute(tail, axis, [(i, (i + 1) % count) for i in range(ends)])]
    all_gather x1, waiting for transfers between devices: 392 us -> 146 us  [body(): lax.all_gather(w_in, ('dp', 'rows'), axis=0, tiled=True)]
    another operation x56, local copies, waits for them, and re-layouts: 0.85 us -> 49.8 us  [kernel_terms(): stacked.append(jnp.stack(row_terms))]
    all_to_all x0 -> x1, starting transfers between devices: none -> 16.5 us  [exchange_gather(): blocks = lax.all_to_all(blocks, mesh_axis, split_axis=0, concat_axis=0)]
    unnamed x162 -> x163, local copies, waits for them, and re-layouts: 33.6 us -> 17.9 us
  transfers between devices with their start and end apart: 8 -> 8, of which waited for: 6 -> 5; matrix products, arithmetic and copies ran while one was open for 5% -> 11% of each run, Pallas kernels for 0% -> 0%
where the time goes in v1:
time: 1070 us; the launch traced here: 1060 us
  waiting for transfers between devices  695 us (65%)
  blocking collectives  135 us (13%)
  local copies, waits for them, and re-layouts  99.9 us (9%)
  other arithmetic  51.8 us (5%)
  matrix products  32.9 us (3%)
  starting transfers between devices  29.9 us (3%)
  between operations  17.6 us (2%)
    ppermute x2, waiting for transfers between devices, padded_2(): lax.ppermute(tail, axis, [(i, (i + 1) % count) for i in range(ends)])  303 us
    psum x1, waiting for transfers between devices, body(): lax.psum((kernel_local, jnp.sum(loss_tok)), ('dp', 'rows'))  234 us
    all_gather x1, waiting for transfers between devices, body(): lax.all_gather(w_in, ('dp', 'rows'), axis=0, tiled=True)  146 us
    psum x1, blocking collectives, body(): lax.psum((kernel_local, jnp.sum(loss_tok)), ('dp', 'rows'))  87.4 us
    another operation x56, local copies, waits for them, and re-layouts, kernel_terms(): stacked.append(jnp.stack(row_terms))  49.8 us
    all_gather x1, blocking collectives, body(): gathered = lax.all_gather(tokens_b[None], 'dp', axis=0, tiled=True)  47.5 us
  transfers between devices with their start and end apart: 8, of which 5 were waited for; matrix products, arithmetic and copies ran while one was open for 11% of the time, Pallas kernels for 0%

profile of v1, /device:TPU:1, one launch (start us, length us, event | category | flops | bytes accessed | tf_op | source)
XLA Modules:
  0.0 1062.1 jit_solution(9285686645904140276)
XLA Ops:
  7.9 6.9 stack.130
  14.8 16.5 %all-to-all-start = ((bf16[256,12,1536]{2,1,0:T(8,128)(2,1)}), bf16[256,12,1536]{2,1,0:T(8,128)(2,1)}, u32[]{:S(2)}, u32[]{:S(2)}) async-start(bf16[256,12,1536]{2,1,0:T(8,128)(2,1)} %stack.130), calls=%async_computation | async-start | bytes 25165824 | tf_op jit(solution)/shard_map/all_to_all | solution.py:17
  31.4 4.1 collective-permute-start.1
  35.5 2.1 collective-permute-start
  40.8 302.6 %collective-permute-done = bf16[1,3,32,1536]{3,2,1,0:T(8,128)(2,1)S(1)} collective-permute-done((bf16[1,3,32,1536]{3,2,1,0:T(8,128)(2,1)S(1)}, bf16[1,3,32,1536]{3,2,1,0:T(8,128)(2,1)S(1)}, u32[]{:S(2)}, u32[]{:S(2)}) %collective-permute-start) | collective-permute-done | bytes 294944 | tf_op jit(solution)/shard_map/ppermute | solution.py:29
  343.5 6.0 collective-permute-done.1
  350.4 13.8 %fusion.157 = (f32[8,32]{1,0:T(8,128)S(1)}, f32[1,8,32,1536]{3,2,1,0:T(8,128)}) fusion(f32[1536]{0:T(1024)S(1)} %get-tuple-element.110, bf16[1,14,38,1536]{3,2,1,0:T(8,128)(2,1)S(1)} %select_maximum_fusion.2, f32[1536]{0:T(1024)S(1)} %get-tuple-element.111, f32[1536]{0:T(1024)S(1)} %get-tuple-element.64, f32[1536]{0:T(1024)S(1)} %get-tuple-element.65, ...), kind=kLoop, calls=%fused_computation.366 | loop fusion | flops 57802496 | bytes 40410112 | tf_op jit(solution)/shard_map/reduce_sum | solution.py:72
  364.3 1.7 multiply_reduce_fusion.1
  366.1 2.8 fusion.136
  368.9 146.0 %all-gather.3.cloned.1.call-done = bf16[256,6,3072]{2,1,0:T(8,128)(2,1)} async-done(((bf16[1,6,3072]{2,1,0:T(8,128)(2,1)}), bf16[256,6,3072]{2,1,0:T(8,128)(2,1)}) %all-gather.3.cloned.1.call-update) | async-done | bytes 9437200 | tf_op jit(solution)/shard_map/all_gather | solution.py:80
  514.9 14.2 %reshape.802 = bf16[1536,3072]{1,0:T(8,128)(2,1)} reshape(bf16[256,6,3072]{2,1,0:T(8,128)(2,1)} %all-gather.3.cloned.1.call-done) | data formatting | bytes 18874368
  529.1 8.5 fusion.141
  537.7 15.0 %reshape.745 = bf16[3072,1536]{1,0:T(8,128)(2,1)} reshape(bf16[256,12,1536]{2,1,0:T(8,128)(2,1)} %all-to-all-done) | data formatting | bytes 18874368 | tf_op jit(solution)/shard_map/reshape | solution.py:18
  552.7 8.5 fusion.7
  561.2 2.7 reshape.746
  563.9 1.8 reduce_sum.544
  565.9 47.5 %all_gather.7 = bf16[16,2,8,1536]{3,2,1,0:T(8,128)(2,1)S(1)} all-gather(bf16[1,2,8,1536]{3,2,1,0:T(8,128)(2,1)S(1)} %fusion.149), channel_id=1, replica_groups=mesh['dp'=16,'rows'=16] {'dp'}, dimensions={0}, use_global_device_ids=true | all-gather | bytes 835584 | tf_op jit(solution)/shard_map/all_gather | solution.py:98
  615.2 1.7 fusion.8
  617.6 87.4 %psum.15 = f32[]{:T(128)} all-reduce(f32[]{:T(128)} %subtract_reduce_fusion), channel_id=1, replica_groups=mesh['dp'=16,'rows'=16] {'dp','rows'}, use_global_device_ids=true, to_apply=%region_62.63 | all-reduce | flops 1 | bytes 8 | tf_op jit(solution)/shard_map/psum | solution.py:161
  705.6 5.8 reduce-scatter.2.cloned.1.call-done
  711.4 1.6 convolution_add_fusion
  714.3 2.3 convert_element_type.1165
  716.6 12.2 %fusion.156 = (f32[256]{0:T(256)S(1)}, f32[256]{0:T(256)S(1)}, f32[256,1536]{1,0:T(8,128)}) fusion(f32[256,1536]{1,0:T(8,128)} %fusion.136, f32[1536]{0:T(1024)S(1)} %copy-done.75, bf16[1536,3072]{1,0:T(8,128)(2,1)} %reshape.802, bf16[256,1536]{1,0:T(8,128)(2,1)} %convert_element_type.1165, bf16[3072,1536]{1,0:T(8,128)(2,1)} %reshape.745, ...), kind=kOutput, calls=%fused_computation.365 | convolution fusion | flops 4841275392 | bytes 25960448 | tf_op jit(solution)/shard_map/dot_general | solution.py:142
  728.9 6.8 fusion.135
  735.7 3.1 fusion.132
  738.8 4.6 fusion.114
  743.4 1.4 broadcast_in_dim.5
  744.8 1.9 reshape_reshape.3
  747.6 4.6 collective-permute-start.3
  752.2 2.4 collective-permute-start.2
  754.8 1.3 stack.140
  756.1 1.3 stack.141
  757.4 1.3 stack.142
  758.7 1.3 stack.143
  760.0 1.3 stack.144
  761.3 1.3 stack.145
  762.5 1.3 stack.146
  763.8 1.3 stack.149
  765.1 1.3 stack.150
  766.4 1.3 stack.151
  767.7 1.3 stack.152
  770.3 1.3 stack.154
  771.6 1.3 stack.155
  772.9 1.3 stack.158
  774.2 1.3 stack.159
  775.5 1.3 stack.160
  776.8 1.3 stack.161
  778.1 1.3 stack.162
  779.4 1.3 stack.163
  780.7 1.3 stack.164
  781.9 1.3 stack.167
  783.3 1.3 stack.168
  785.8 1.3 stack.170
  787.1 1.3 stack.171
  788.4 1.3 stack.172
  789.7 1.3 stack.173
  791.0 1.3 stack.176
  792.3 1.3 stack.177
  793.6 1.3 stack.178
  794.9 1.3 stack.179
  796.2 1.3 stack.180
  806.5 12.1 %add_convert_fusion = bf16[1,8,32,1536]{3,2,1,0:T(8,128)(2,1)} fusion(f32[1,8,32,1536]{3,2,1,0:T(8,128)S(1)} %reshape_reshape.3, bf16[1,8,32,1536]{3,2,1,0:T(8,128)(2,1)S(1)} %bitcast.108, bf16[1,3,32,1536]{3,2,1,0:T(8,128)(2,1)S(1)} %collective-permute-done.3, bf16[1,3,32,1536]{3,2,1,0:T(8,128)(2,1)S(1)} %collective-permute-done.2, ...), kind=kLoop, calls=%fused_computation.250 | loop fusion | flops 60555264 | bytes 37066752 | tf_op jit(solution)/shard_map/convert_element_type | solution.py:157
  818.6 234.1 %all-reduce.4.cloned.1.call-done = f32[7,7,1536]{2,1,0:T(8,128)} async-done(((f32[7,7,1536]{2,1,0:T(8,128)}), f32[7,7,1536]{2,1,0:T(8,128)}) %all-reduce.4.cloned.1.call-update) | async-done | bytes 301072 | tf_op jit(solution)/shard_map/psum | solution.py:161
  1052.7 1.7 copy.48
  (229 shorter events, 19.9 us)
Async XLA Ops:
  7.2 507.7 %all-gather.3.cloned.1.call-start = ((), (), s32[]{:S(2)}) async-start(), calls=%async_computation.4 | async-start | bytes 12632064 | tf_op jit(solution)/shard_map/all_gather | solution.py:80
  14.8 16.6 %copy-start.4 = (bf16[1,8,32,1536]{3,2,1,0:T(8,128)(2,1)S(1)}, bf16[1,8,32,1536]{3,2,1,0:T(8,128)(2,1)}, u32[]{:S(2)}) copy-start(bf16[1,8,32,1536]{3,2,1,0:T(8,128)(2,1)} %param.8) | copy-start | bytes 2359300
  14.8 22.9 %copy-start.76 = (s32[16]{0:T(128)S(1)}, s32[16]{0:T(128)}, u32[]{:S(2)}) copy-start(s32[16]{0:T(128)} %param.14) | copy-start | bytes 196
  14.8 24.2 %copy-start.73 = (s32[1,2,8,8]{3,2,1,0:T(8,128)S(1)}, s32[1,2,8,8]{3,2,1,0:T(8,128)}, u32[]{:S(2)}) copy-start(s32[1,2,8,8]{3,2,1,0:T(8,128)} %param.15) | copy-start | bytes 1540
  14.8 24.3 %copy-start.8 = (bf16[7,7,1536]{2,1,0:T(8,128)(2,1)S(1)}, bf16[7,7,1536]{2,1,0:T(8,128)(2,1)}, u32[]{:S(2)}) copy-start(bf16[7,7,1536]{2,1,0:T(8,128)(2,1)} %param.9) | copy-start | bytes 451588
  14.8 522.9 %all-to-all-start = ((bf16[256,12,1536]{2,1,0:T(8,128)(2,1)}), bf16[256,12,1536]{2,1,0:T(8,128)(2,1)}, u32[]{:S(2)}, u32[]{:S(2)}) async-start(bf16[256,12,1536]{2,1,0:T(8,128)(2,1)} %stack.130), calls=%async_computation | async-start | bytes 25165824 | tf_op jit(solution)/shard_map/all_to_all | solution.py:17
  31.3 680.0 %reduce-scatter.2.cloned.1.call-start = ((), (), s32[]{:S(2)}) async-start(), calls=%async_computation.2 | async-start | bytes 835584 | tf_op jit(solution)/shard_map/reduce_scatter | solution.py:126
  31.4 318.1 %collective-permute-start.1 = (bf16[1,3,32,1536]{3,2,1,0:T(8,128)(2,1)S(1)}, bf16[1,3,32,1536]{3,2,1,0:T(8,128)(2,1)S(1)}, u32[]{:S(2)}, u32[]{:S(2)}) collective-permute-start(bf16[1,3,32,1536]{3,2,1,0:T(8,128)(2,1)S(1)} %get-tuple-element.120), channel_id=1, source_target_pairs={{1,0},{2,1},{3,2},{4,3},{5,4},{6,5},{7,6},{8,7},{9,8},{10,9},{11,1... | collective-permute-start | bytes 884744 | tf_op jit(solution)/shard_map/ppermute | solution.py:31
  35.5 307.8 %collective-permute-start = (bf16[1,3,32,1536]{3,2,1,0:T(8,128)(2,1)S(1)}, bf16[1,3,32,1536]{3,2,1,0:T(8,128)(2,1)S(1)}, u32[]{:S(2)}, u32[]{:S(2)}) collective-permute-start(bf16[1,3,32,1536]{3,2,1,0:T(8,128)(2,1)S(1)} %get-tuple-element.119), channel_id=1, source_target_pairs={{0,1},{1,2},{2,3},{3,4},{4,5},{5,6},{6,7},{7,8},{8,9},{9,10},{10,1... | collective-permute-start | bytes 884744 | tf_op jit(solution)/shard_map/ppermute | solution.py:29
  40.2 309.9 %copy-start.10 = (f32[1536]{0:T(1024)}, f32[1536]{0:T(1024)S(1)}, u32[]{:S(2)}) copy-start(f32[1536]{0:T(1024)S(1)} %get-tuple-element.70) | copy-start | bytes 18436
  40.2 309.9 %copy-start.12 = (f32[1536]{0:T(1024)}, f32[1536]{0:T(1024)S(1)}, u32[]{:S(2)}) copy-start(f32[1536]{0:T(1024)S(1)} %get-tuple-element.71) | copy-start | bytes 18436
  40.2 309.9 %copy-start.14 = (f32[1536]{0:T(1024)}, f32[1536]{0:T(1024)S(1)}, u32[]{:S(2)}) copy-start(f32[1536]{0:T(1024)S(1)} %get-tuple-element.72) | copy-start | bytes 18436
  40.2 309.9 %copy-start.16 = (f32[1536]{0:T(1024)}, f32[1536]{0:T(1024)S(1)}, u32[]{:S(2)}) copy-start(f32[1536]{0:T(1024)S(1)} %get-tuple-element.73) | copy-start | bytes 18436
  40.2 309.9 %copy-start.18 = (f32[1536]{0:T(1024)}, f32[1536]{0:T(1024)S(1)}, u32[]{:S(2)}) copy-start(f32[1536]{0:T(1024)S(1)} %get-tuple-element.74) | copy-start | bytes 18436
  40.2 309.9 %copy-start.20 = (f32[1536]{0:T(1024)}, f32[1536]{0:T(1024)S(1)}, u32[]{:S(2)}) copy-start(f32[1536]{0:T(1024)S(1)} %get-tuple-element.75) | copy-start | bytes 18436
  40.2 309.9 %copy-start.22 = (f32[1536]{0:T(1024)}, f32[1536]{0:T(1024)S(1)}, u32[]{:S(2)}) copy-start(f32[1536]{0:T(1024)S(1)} %get-tuple-element.76) | copy-start | bytes 18436
  40.2 309.9 %copy-start.24 = (f32[1536]{0:T(1024)}, f32[1536]{0:T(1024)S(1)}, u32[]{:S(2)}) copy-start(f32[1536]{0:T(1024)S(1)} %get-tuple-element.77) | copy-start | bytes 18436
  40.3 309.9 %copy-start.26 = (f32[1536]{0:T(1024)}, f32[1536]{0:T(1024)S(1)}, u32[]{:S(2)}) copy-start(f32[1536]{0:T(1024)S(1)} %get-tuple-element.78) | copy-start | bytes 18436
  40.3 309.9 %copy-start.28 = (f32[1536]{0:T(1024)}, f32[1536]{0:T(1024)S(1)}, u32[]{:S(2)}) copy-start(f32[1536]{0:T(1024)S(1)} %get-tuple-element.79) | copy-start | bytes 18436
  40.3 309.9 %copy-start.30 = (f32[1536]{0:T(1024)}, f32[1536]{0:T(1024)S(1)}, u32[]{:S(2)}) copy-start(f32[1536]{0:T(1024)S(1)} %get-tuple-element.80) | copy-start | bytes 18436
  40.3 309.9 %copy-start.32 = (f32[1536]{0:T(1024)}, f32[1536]{0:T(1024)S(1)}, u32[]{:S(2)}) copy-start(f32[1536]{0:T(1024)S(1)} %get-tuple-element.81) | copy-start | bytes 18436
  40.6 309.6 %copy-start.34 = (f32[1536]{0:T(1024)}, f32[1536]{0:T(1024)S(1)}, u32[]{:S(2)}) copy-start(f32[1536]{0:T(1024)S(1)} %get-tuple-element.82) | copy-start | bytes 18436
  40.6 309.6 %copy-start.36 = (f32[1536]{0:T(1024)}, f32[1536]{0:T(1024)S(1)}, u32[]{:S(2)}) copy-start(f32[1536]{0:T(1024)S(1)} %get-tuple-element.83) | copy-start | bytes 18436
  40.6 309.6 %copy-start.38 = (f32[1536]{0:T(1024)}, f32[1536]{0:T(1024)S(1)}, u32[]{:S(2)}) copy-start(f32[1536]{0:T(1024)S(1)} %get-tuple-element.84) | copy-start | bytes 18436
  40.6 309.6 %copy-start.40 = (f32[1536]{0:T(1024)}, f32[1536]{0:T(1024)S(1)}, u32[]{:S(2)}) copy-start(f32[1536]{0:T(1024)S(1)} %get-tuple-element.85) | copy-start | bytes 18436
  40.7 309.6 %copy-start.42 = (f32[1536]{0:T(1024)}, f32[1536]{0:T(1024)S(1)}, u32[]{:S(2)}) copy-start(f32[1536]{0:T(1024)S(1)} %get-tuple-element.86) | copy-start | bytes 18436
  40.7 309.6 %copy-start.44 = (f32[1536]{0:T(1024)}, f32[1536]{0:T(1024)S(1)}, u32[]{:S(2)}) copy-start(f32[1536]{0:T(1024)S(1)} %get-tuple-element.87) | copy-start | bytes 18436
  40.7 309.6 %copy-start.46 = (f32[1536]{0:T(1024)}, f32[1536]{0:T(1024)S(1)}, u32[]{:S(2)}) copy-start(f32[1536]{0:T(1024)S(1)} %get-tuple-element.88) | copy-start | bytes 18436
  40.7 309.6 %copy-start.48 = (f32[1536]{0:T(1024)}, f32[1536]{0:T(1024)S(1)}, u32[]{:S(2)}) copy-start(f32[1536]{0:T(1024)S(1)} %get-tuple-element.89) | copy-start | bytes 18436
  40.7 309.6 %copy-start.50 = (f32[1536]{0:T(1024)}, f32[1536]{0:T(1024)S(1)}, u32[]{:S(2)}) copy-start(f32[1536]{0:T(1024)S(1)} %get-tuple-element.90) | copy-start | bytes 18436
  40.7 309.6 %copy-start.52 = (f32[1536]{0:T(1024)}, f32[1536]{0:T(1024)S(1)}, u32[]{:S(2)}) copy-start(f32[1536]{0:T(1024)S(1)} %get-tuple-element.91) | copy-start | bytes 18436
  40.7 309.6 %copy-start.54 = (f32[1536]{0:T(1024)}, f32[1536]{0:T(1024)S(1)}, u32[]{:S(2)}) copy-start(f32[1536]{0:T(1024)S(1)} %get-tuple-element.92) | copy-start | bytes 18436
  40.7 309.6 %copy-start.56 = (f32[1536]{0:T(1024)}, f32[1536]{0:T(1024)S(1)}, u32[]{:S(2)}) copy-start(f32[1536]{0:T(1024)S(1)} %get-tuple-element.93) | copy-start | bytes 18436
  40.7 309.6 %copy-start.58 = (f32[1536]{0:T(1024)}, f32[1536]{0:T(1024)S(1)}, u32[]{:S(2)}) copy-start(f32[1536]{0:T(1024)S(1)} %get-tuple-element.94) | copy-start | bytes 18436
  40.7 309.6 %copy-start.60 = (f32[1536]{0:T(1024)}, f32[1536]{0:T(1024)S(1)}, u32[]{:S(2)}) copy-start(f32[1536]{0:T(1024)S(1)} %get-tuple-element.95) | copy-start | bytes 18436
  40.8 309.6 %copy-start.62 = (f32[1536]{0:T(1024)}, f32[1536]{0:T(1024)S(1)}, u32[]{:S(2)}) copy-start(f32[1536]{0:T(1024)S(1)} %get-tuple-element.96) | copy-start | bytes 18436
  40.8 309.6 %copy-start.64 = (f32[1536]{0:T(1024)}, f32[1536]{0:T(1024)S(1)}, u32[]{:S(2)}) copy-start(f32[1536]{0:T(1024)S(1)} %get-tuple-element.97) | copy-start | bytes 18436
  40.8 309.6 %copy-start.66 = (f32[1536]{0:T(1024)}, f32[1536]{0:T(1024)S(1)}, u32[]{:S(2)}) copy-start(f32[1536]{0:T(1024)S(1)} %get-tuple-element.98) | copy-start | bytes 18436
  40.8 309.6 %copy-start.68 = (f32[1536]{0:T(1024)}, f32[1536]{0:T(1024)S(1)}, u32[]{:S(2)}) copy-start(f32[1536]{0:T(1024)S(1)} %get-tuple-element.99) | copy-start | bytes 18436
  40.8 309.6 %copy-start.70 = (f32[1536]{0:T(1024)}, f32[1536]{0:T(1024)S(1)}, u32[]{:S(2)}) copy-start(f32[1536]{0:T(1024)S(1)} %get-tuple-element.100) | copy-start | bytes 18436
  343.4 6.2 copy-start.5
  343.5 6.9 copy-start.2
  368.9 160.2 %copy-start.75 = (f32[1536]{0:T(1024)S(1)}, f32[1536]{0:T(1024)}, u32[]{:S(2)}) copy-start(f32[1536]{0:T(1024)} %param.10) | copy-start | bytes 18436
  537.7 15.0 %copy-start.72 = (f32[1536]{0:T(1024)S(1)}, f32[1536]{0:T(1024)}, u32[]{:S(2)}) copy-start(f32[1536]{0:T(1024)} %param.11) | copy-start | bytes 18436
  563.9 50.9 %copy-start.74 = (f32[9]{0:T(128)S(1)}, f32[9]{0:T(128)}, u32[]{:S(2)}) copy-start(f32[9]{0:T(128)} %compare_convert_fusion) | copy-start | bytes 112
  613.4 0.9 copy-start.7
  616.9 435.8 %all-reduce.4.cloned.1.call-start = ((), (), s32[]{:S(2)}) async-start(), calls=%async_computation.3 | async-start | bytes 688128 | tf_op jit(solution)/shard_map/psum | solution.py:161
  728.8 6.8 copy-start.3
  728.9 6.8 copy-start.6
  735.7 3.1 copy-start
  744.8 1.9 copy-start.1
  747.6 58.0 %collective-permute-start.3 = (bf16[1,3,32,1536]{3,2,1,0:T(8,128)(2,1)}, bf16[1,3,32,1536]{3,2,1,0:T(8,128)(2,1)S(1)}, u32[]{:S(2)}, u32[]{:S(2)}) collective-permute-start(bf16[1,3,32,1536]{3,2,1,0:T(8,128)(2,1)} %get-tuple-element.116), channel_id=1, source_target_pairs={{1,0},{2,1},{3,2},{4,3},{5,4},{6,5},{7,6},{8,7},{9,8},{10,9},{11,1... | collective-permute-start | bytes 884744 | tf_op jit(solution)/shard_map/ppermute | solution.py:31
  752.2 53.5 %collective-permute-start.2 = (bf16[1,3,32,1536]{3,2,1,0:T(8,128)(2,1)}, bf16[1,3,32,1536]{3,2,1,0:T(8,128)(2,1)S(1)}, u32[]{:S(2)}, u32[]{:S(2)}) collective-permute-start(bf16[1,3,32,1536]{3,2,1,0:T(8,128)(2,1)} %get-tuple-element.115), channel_id=1, source_target_pairs={{0,1},{1,2},{2,3},{3,4},{4,5},{5,6},{6,7},{7,8},{8,9},{9,10},{10,1... | collective-permute-start | bytes 884744 | tf_op jit(solution)/shard_map/ppermute | solution.py:29
  805.3 0.9 copy-start.11
  805.3 0.9 copy-start.13
  805.3 0.9 copy-start.15
  805.3 0.9 copy-start.17
  805.4 0.9 copy-start.19
  805.4 0.9 copy-start.21
  805.4 0.9 copy-start.23
  805.4 0.9 copy-start.25
  805.4 0.9 copy-start.27
  805.4 0.9 copy-start.29
  805.4 0.9 copy-start.31
  (21 other events, 17.9 us)
Sparse Core Ops, SparseCore 0:
  9.9 505.0 all-gather.2
  617.0 94.2 reduce-scatter.1
  805.4 247.1 all-reduce.3
